TPU v7x, 32 devices: a whole 2x2x4 slice. The times are simulated.
32 devices in a mesh: grp: 2 (over y), ctx: 4 (over z), tp: 2 (over x), sub: 2 (over core).
Axes of the slice: x: 2, y: 2, z: 4, core: 2. Of those that a mesh axis runs over, the one named last changes fastest.
Arguments:
- context: bfloat16 [3072, 2048], P(('grp', 'ctx'), ('tp', 'sub')), parts along dimension 0, may hold values from -24 to 24
- context_pos: int32 [3072], P(('grp', 'ctx')), parts along dimension 0, may hold values from 0 to 1535, each once
- latent_in: bfloat16 [64, 2048], P(('grp', 'ctx')), parts along dimension 0, may hold values from -24 to 24
- latent_start: int32 [2], P('grp'), parts along dimension 0, may hold values from 768 to 1504
- ctx_gain: float32 [2048], replicated, may hold values from 0.25 to 1.75
- lat_gain: float32 [2048], replicated, may hold values from 0.25 to 1.75
- mid_gain: float32 [2048], replicated, may hold values from 0.25 to 1.75
- cross_q: bfloat16 [2048, 2048], P('ctx', ('tp', 'sub')), may hold values from -2 to 2
- cross_k: bfloat16 [2048, 2048], P('ctx', ('tp', 'sub')), may hold values from -2 to 2
- cross_v: bfloat16 [2048, 2048], P('ctx', ('tp', 'sub')), may hold values from -0.125 to 0.125
- cross_out: bfloat16 [2048, 2048], P('ctx', ('tp', 'sub')), may hold values from -0.125 to 0.125
- self_qkv: bfloat16 [2048, 3, 2048], P('ctx', None, ('tp', 'sub')), may hold values from -2 to 2
- self_out: bfloat16 [2048, 2048], P('ctx', ('tp', 'sub')), may hold values from -0.125 to 0.125
Outputs:
- latent_out: bfloat16 [64, 2048], P(('grp', 'ctx'), ('tp', 'sub')), parts along dimension 0
There are 2 independent parts, one for each index of `grp`. A program takes and returns all parts, laid end to end along the dimension named above; an argument that names none is the same for every part. Nothing has to cross between parts.
Inputs may be any that keep to these rules, and one draw needn't show every extreme that they name: context_pos holds each of 0 to 1535 once.
All inputs are finite; a program needn't handle non-finite values.
Results may differ from a plain program's by a relative error of at most 0.035.
Values may be sent and summed in bfloat16 or wider, within the bound.
A program may use at most 64 MiB of HBM per device.

v0:
```python
import math
import jax
import jax.numpy as jnp
from jax import lax
from jax.sharding import PartitionSpec as P

DH = 128
EPS = 1e-05
NEG = -1e30
HEADS_AXES = ("tp", "sub")


def contract_last(left, right):
    return lax.dot_general(
        left, right, (((1,), (1,)), ((), ())), preferred_element_type=jnp.float32
    )


def summed_over(partial, axis):
    everything = lax.all_gather(partial.astype(jnp.bfloat16), axis)
    return jnp.sum(everything.astype(jnp.float32), axis=0)


def on_device(
    context,
    context_pos,
    latent_in,
    latent_start,
    ctx_gain,
    lat_gain,
    mid_gain,
    cross_q,
    cross_k,
    cross_v,
    cross_out,
    self_qkv,
    self_out,
):
    rows, width = latent_in.shape
    depth, columns = cross_q.shape
    shards = lax.axis_size("ctx")
    heads = columns // DH
    latents = rows * shards
    own = lax.axis_index("ctx")
    mine = lambda array: lax.dynamic_slice_in_dim(array, own * depth, depth, array.ndim - 1)
    whole = lax.all_gather(context, HEADS_AXES, axis=1, tiled=True)
    all_latents = lax.all_gather(latent_in, "ctx", axis=0, tiled=True).astype(jnp.float32)
    lat_scale = lax.rsqrt(jnp.mean(all_latents * all_latents, axis=1, keepdims=True) + EPS)
    lat_part = mine(all_latents)
    normed_lat = (lat_part * lat_scale * mine(lat_gain)).astype(jnp.bfloat16)
    queries = summed_over(
        jnp.dot(normed_lat, cross_q, preferred_element_type=jnp.float32), "ctx"
    ).astype(jnp.bfloat16)
    split = [slice(head * DH, head * DH + DH) for head in range(heads)]
    absorbed = jnp.concatenate(
        [contract_last(queries[:, cut], cross_k[:, cut]) for cut in split], axis=0
    )
    absorbed = (absorbed * (mine(ctx_gain) * (1.0 / math.sqrt(DH)))).astype(jnp.bfloat16)
    absorbed = lax.all_gather(absorbed, "ctx", axis=1, tiled=True)
    wide = whole.astype(jnp.float32)
    token_scale = lax.rsqrt(jnp.mean(wide * wide, axis=1) + EPS)
    scores = contract_last(absorbed, whole) * token_scale[None, :]
    query_pos = latent_start[0] + jnp.arange(latents, dtype=jnp.int32)
    allowed = jnp.tile(context_pos[None, :] <= query_pos[:, None], (heads, 1))
    scores = jnp.where(allowed, scores, NEG)
    top = jnp.max(scores, axis=1, keepdims=True)
    weights = jnp.where(allowed, jnp.exp(scores - top), 0.0)
    total = jnp.sum(weights, axis=1, keepdims=True)
    mixed = jnp.dot(
        (weights * token_scale[None, :]).astype(jnp.bfloat16),
        whole,
        preferred_element_type=jnp.float32,
    ).astype(jnp.bfloat16)
    mixed = lax.all_to_all(
        mixed.reshape(heads * latents, shards, depth), "ctx", split_axis=1, concat_axis=0
    ).reshape(shards, heads * latents, depth)
    stats = lax.all_gather(jnp.concatenate([top, total], axis=1), "ctx")
    tops, totals = (stats[:, :, :1], stats[:, :, 1:])
    factors = jnp.exp(tops - jnp.max(tops, axis=0))
    mixed = jnp.sum(mixed.astype(jnp.float32) * factors, axis=0) / jnp.sum(totals * factors, axis=0)
    mixed = (mixed * mine(ctx_gain)).astype(jnp.bfloat16)
    attended = jnp.concatenate(
        [
            jnp.dot(
                mixed[head * latents : (head + 1) * latents],
                cross_v[:, cut],
                preferred_element_type=jnp.float32,
            )
            for head, cut in enumerate(split)
        ],
        axis=1,
    )
    attended = summed_over(attended, "ctx").astype(jnp.bfloat16)
    cross_sum = summed_over(contract_last(attended, cross_out), HEADS_AXES)
    hidden = (lat_part + cross_sum).astype(jnp.bfloat16).astype(jnp.float32)
    squares = jnp.sum(lax.all_gather(jnp.sum(hidden * hidden, axis=1), "ctx"), axis=0)
    hidden_scale = lax.rsqrt(squares / width + EPS)
    projected = jnp.dot(
        (hidden * mine(mid_gain)).astype(jnp.bfloat16),
        self_qkv.reshape(depth, 3 * columns),
        preferred_element_type=jnp.float32,
    )
    projected = summed_over(projected, "ctx") * hidden_scale[:, None]
    projected = projected.astype(jnp.bfloat16).reshape(latents, 3, columns)
    index = jnp.arange(latents, dtype=jnp.int32)
    causal = index[None, :] <= index[:, None]
    parts = []
    for cut in split:
        scores = contract_last(projected[:, 0, cut], projected[:, 1, cut]) * (1.0 / math.sqrt(DH))
        scores = jnp.where(causal, scores, NEG)
        weights = jnp.where(causal, jnp.exp(scores - jnp.max(scores, axis=1, keepdims=True)), 0.0)
        numerator = jnp.dot(
            weights.astype(jnp.bfloat16), projected[:, 2, cut], preferred_element_type=jnp.float32
        )
        parts.append(numerator / jnp.sum(weights, axis=1, keepdims=True))
    attended_self = jnp.concatenate(parts, axis=1).astype(jnp.bfloat16)
    self_sum = summed_over(contract_last(attended_self, self_out), HEADS_AXES)
    result = (hidden + self_sum).astype(jnp.bfloat16)
    result = lax.all_to_all(
        result.reshape(shards, rows, depth), "ctx", split_axis=0, concat_axis=1
    ).reshape(rows, width)
    return lax.dynamic_slice_in_dim(result, lax.axis_index(HEADS_AXES) * columns, columns, 1)


def solution(mesh):
    return jax.shard_map(
        on_device,
        mesh=mesh,
        in_specs=(
            P(("grp", "ctx"), ("tp", "sub")),
            P(("grp", "ctx")),
            P(("grp", "ctx"), None),
            P("grp"),
            P(),
            P(),
            P(),
            P("ctx", ("tp", "sub")),
            P("ctx", ("tp", "sub")),
            P("ctx", ("tp", "sub")),
            P("ctx", ("tp", "sub")),
            P("ctx", None, ("tp", "sub")),
            P("ctx", ("tp", "sub")),
        ),
        out_specs=P(("grp", "ctx"), ("tp", "sub")),
        check_vma=False,
    )
```

profile of v0, /device:TPU:0, one launch (start us, length us, event | category | flops | bytes accessed | tf_op | source)
XLA Modules:
  0.0 152.7 jit_solution(14311558146944119064)
XLA Ops:
  6.5 0.7 all-gather.8.cloned.1.call-update
  7.3 15.3 %all_gather.49 = bf16[32,2048]{1,0:T(8,128)(2,1)S(1)} all-gather(bf16[8,2048]{1,0:T(8,128)(2,1)} %param.15), channel_id=1, replica_groups=mesh['grp'=2,'ctx'=4,'tp'=2,'sub'=2] {'ctx'}, dimensions={0}, use_global_device_ids=true | all-gather | bytes 163840 | tf_op jit(solution)/shard_map/all_gather | solution.py:47
  23.4 0.8 dynamic_slice.17
  24.4 13.7 %all-gather = bf16[128,512]{1,0:T(8,128)(2,1)S(1)} all-gather(bf16[32,512]{1,0:T(8,128)(2,1)S(1)} %convolution_convert_fusion.4), channel_id=2, replica_groups=mesh['grp'=2,'ctx'=4,'tp'=2,'sub'=2] {'ctx'}, dimensions={0}, use_global_device_ids=true | all-gather | bytes 163840 | tf_op jit(solution)/shard_map/all_gather | solution.py:20
  38.1 0.8 broadcast_multiply_fusion
  39.5 15.5 %all_gather.52 = bf16[128,2048]{1,0:T(8,128)(2,1)S(1)} all-gather(bf16[128,512]{1,0:T(8,128)(2,1)S(1)} %fusion.14), channel_id=1, replica_groups=mesh['grp'=2,'ctx'=4,'tp'=2,'sub'=2] {'ctx'}, dimensions={1}, use_global_device_ids=true | all-gather | bytes 655360 | tf_op jit(solution)/shard_map/all_gather | solution.py:59
  55.1 1.9 %multiply_reduce_fusion = f32[384]{0:T(512)S(1)} fusion(bf16[384,2048]{1,0:T(8,128)(2,1)} %all-gather.8.cloned.1.call-done), kind=kLoop, calls=%fused_computation | loop fusion | flops 2358912 | bytes 1574400 | tf_op jit(solution)/shard_map/reduce_sum | solution.py:61
  57.1 0.7 fusion.104
  58.8 0.9 copy.17
  59.7 4.7 %all-to-all-start = ((bf16[1,128,4,512]{3,1,0,2:T(8,128)(2,1)}), bf16[1,128,4,512]{3,1,0,2:T(8,128)(2,1)S(1)}, u32[]{:S(2)}, u32[]{:S(2)}) async-start(bf16[1,128,4,512]{3,1,0,2:T(8,128)(2,1)} %copy.17), calls=%async_computation | async-start | bytes 1048576 | tf_op jit(solution)/shard_map/all_to_all | solution.py:74
  64.4 0.8 dynamic_slice.19
  65.2 1.7 %copy.18 = bf16[512,3,512]{0,2,1:T(8,128)(2,1)S(1)} copy(bf16[512,3,512]{2,0,1:T(8,128)(2,1)} %param.24) | data formatting | bytes 3145728 | tf_op args[11]
  68.2 11.4 %all-gather.1 = f32[512,2]{0,1:T(2,128)S(1)} all-gather(f32[128,2]{0,1:T(2,128)S(1)} %pad_maximum_fusion.1), channel_id=3, replica_groups=mesh['grp'=2,'ctx'=4,'tp'=2,'sub'=2] {'ctx'}, dimensions={0}, use_global_device_ids=true | all-gather | bytes 5120 | tf_op jit(solution)/shard_map/all_gather | solution.py:77
  80.0 1.0 fusion.10
  81.0 1.0 fusion.11
  82.0 1.0 fusion.12
  83.1 1.0 fusion.9
  84.2 13.4 %all_gather.56 = bf16[4,32,512]{2,1,0:T(8,128)(2,1)S(1)} all-gather(bf16[1,32,512]{2,1,0:T(8,128)(2,1)S(1)} %pad_maximum_fusion), channel_id=1, replica_groups=mesh['grp'=2,'ctx'=4,'tp'=2,'sub'=2] {'ctx'}, dimensions={0}, use_global_device_ids=true | all-gather | bytes 163840 | tf_op jit(solution)/shard_map/all_gather | solution.py:20
  97.8 5.4 %all-gather.2 = bf16[128,512]{1,0:T(8,128)(2,1)S(1)} all-gather(bf16[32,512]{1,0:T(8,128)(2,1)S(1)} %convolution_convert_fusion.3), channel_id=4, replica_groups=mesh['grp'=2,'ctx'=4,'tp'=2,'sub'=2] {'tp','sub'}, dimensions={0}, use_global_device_ids=true | all-gather | bytes 163840 | tf_op jit(solution)/shard_map/all_gather | solution.py:20
  104.0 15.4 %all-gather.3 = bf16[128,1536]{1,0:T(8,128)(2,1)S(1)} all-gather(bf16[32,1536]{1,0:T(8,128)(2,1)S(1)} %convolution_convert_fusion.1), channel_id=5, replica_groups=mesh['grp'=2,'ctx'=4,'tp'=2,'sub'=2] {'ctx'}, dimensions={0}, use_global_device_ids=true | all-gather | bytes 491520 | tf_op jit(solution)/shard_map/all_gather | solution.py:20
  119.8 8.3 %all-reduce = f32[128]{0:T(128)S(1)} all-reduce(f32[128]{0:T(128)S(1)} %dynamic-update-slice), channel_id=6, replica_groups=mesh['grp'=2,'ctx'=4,'tp'=2,'sub'=2] {'ctx'}, use_global_device_ids=true, to_apply=%add | all-reduce | flops 128 | bytes 1024
  130.3 5.4 %all-gather.5 = bf16[128,512]{1,0:T(8,128)(2,1)S(1)} all-gather(bf16[32,512]{1,0:T(8,128)(2,1)S(1)} %convolution_convert_fusion.2), channel_id=7, replica_groups=mesh['grp'=2,'ctx'=4,'tp'=2,'sub'=2] {'tp','sub'}, dimensions={0}, use_global_device_ids=true | all-gather | bytes 163840 | tf_op jit(solution)/shard_map/all_gather | solution.py:20
  136.4 3.3 %all-to-all-start.1 = ((bf16[4,8,1,512]{3,1,2,0:T(8,128)(2,1)}), bf16[4,8,1,512]{3,1,2,0:T(8,128)(2,1)S(1)}, u32[]{:S(2)}, u32[]{:S(2)}) async-start(bf16[4,8,1,512]{3,1,2,0:T(8,128)(2,1)} %fusion.31), calls=%async_computation.1 | async-start | bytes 65536 | tf_op jit(solution)/shard_map/all_to_all | solution.py:119
  139.6 5.7 %all-to-all-done.1 = bf16[4,8,1,512]{3,1,2,0:T(8,128)(2,1)S(1)} async-done(((bf16[4,8,1,512]{3,1,2,0:T(8,128)(2,1)}), bf16[4,8,1,512]{3,1,2,0:T(8,128)(2,1)S(1)}, u32[]{:S(2)}, u32[]{:S(2)}) %all-to-all-start.1) | async-done | bytes 32800 | tf_op jit(solution)/shard_map/all_to_all | solution.py:119
  (72 shorter events, 7.9 us)
Async XLA Ops:
  6.5 17.6 %copy-start = (bf16[512,512]{1,0:T(8,128)(2,1)S(1)}, bf16[512,512]{1,0:T(8,128)(2,1)}, u32[]{:S(2)}) copy-start(bf16[512,512]{1,0:T(8,128)(2,1)} %param.20) | copy-start | bytes 1572868
  6.5 32.3 %copy-start.4 = (bf16[512,512]{1,0:T(8,128)(2,1)S(1)}, bf16[512,512]{1,0:T(8,128)(2,1)}, u32[]{:S(2)}) copy-start(bf16[512,512]{1,0:T(8,128)(2,1)} %param.21) | copy-start | bytes 1572868
  6.5 48.6 %all-gather.8.cloned.1.call-start = ((), (), s32[]{:S(2)}) async-start(), calls=%async_computation.2 | async-start | bytes 1966080 | tf_op jit(solution)/shard_map/all_gather | solution.py:46
  22.7 32.4 %copy-start.5 = (s32[384]{0:T(512)S(1)}, s32[384]{0:T(512)}, u32[]{:S(2)}) copy-start(s32[384]{0:T(512)} %param.14) | copy-start | bytes 4612
  55.1 2.0 %copy-start.1 = (bf16[384,2048]{1,0:T(8,128)(2,1)S(1)}, bf16[384,2048]{1,0:T(8,128)(2,1)}, u32[]{:S(2)}) copy-start(bf16[384,2048]{1,0:T(8,128)(2,1)} %all-gather.8.cloned.1.call-done) | copy-start | bytes 4718596
  59.7 20.0 %all-to-all-start = ((bf16[1,128,4,512]{3,1,0,2:T(8,128)(2,1)}), bf16[1,128,4,512]{3,1,0,2:T(8,128)(2,1)S(1)}, u32[]{:S(2)}, u32[]{:S(2)}) async-start(bf16[1,128,4,512]{3,1,0,2:T(8,128)(2,1)} %copy.17), calls=%async_computation | async-start | bytes 1048576 | tf_op jit(solution)/shard_map/all_to_all | solution.py:74
  65.2 1.8 %copy-start.6 = (u32[32]{0:T(128)S(1)}, u32[32]{0:T(128)}, u32[]{:S(2)}) copy-start(u32[32]{0:T(128)} %constant.45) | copy-start | bytes 388
  66.9 30.7 %copy-start.2 = (bf16[512,512]{1,0:T(8,128)(2,1)S(1)}, bf16[512,512]{1,0:T(8,128)(2,1)}, u32[]{:S(2)}) copy-start(bf16[512,512]{1,0:T(8,128)(2,1)} %param.23) | copy-start | bytes 1572868
  104.0 26.0 %copy-start.3 = (bf16[512,512]{1,0:T(8,128)(2,1)S(1)}, bf16[512,512]{1,0:T(8,128)(2,1)}, u32[]{:S(2)}) copy-start(bf16[512,512]{1,0:T(8,128)(2,1)} %param.25) | copy-start | bytes 1572868
  136.4 8.9 %all-to-all-start.1 = ((bf16[4,8,1,512]{3,1,2,0:T(8,128)(2,1)}), bf16[4,8,1,512]{3,1,2,0:T(8,128)(2,1)S(1)}, u32[]{:S(2)}, u32[]{:S(2)}) async-start(bf16[4,8,1,512]{3,1,2,0:T(8,128)(2,1)} %fusion.31), calls=%async_computation.1 | async-start | bytes 65536 | tf_op jit(solution)/shard_map/all_to_all | solution.py:119
Sparse Core Ops, SparseCore 0:
  8.9 22.3 all-gather.7
where the time goes:
time: 153 us
  blocking collectives  104 us (68%)
  between operations  14.9 us (10%)
  matrix products  8.52 us (6%)
  starting transfers between devices  8.01 us (5%)
  local copies, waits for them, and re-layouts  6.4 us (4%)
  waiting for transfers between devices  6.38 us (4%)
  other arithmetic  4.64 us (3%)
    all_gather x5, blocking collectives, summed_over(): everything = lax.all_gather(partial.astype(jnp.bfloat16), axis)  53.4 us
    all_gather x1, blocking collectives, on_device(): absorbed = lax.all_gather(absorbed, 'ctx', axis=1, tiled=True)  15.5 us
    all_gather x1, blocking collectives, on_device(): lax.all_gather(latent_in, 'ctx', axis=0, tiled=True).astype(jnp.float32)  15.3 us
    all_gather x1, blocking collectives, on_device(): stats = lax.all_gather(jnp.concatenate([top, total], axis=1), 'ctx')  11.4 us
    unnamed x1, blocking collectives  8.34 us
    all_to_all x1, waiting for transfers between devices, on_device(): lax.all_to_all(result.reshape(shards, rows, depth), 'ctx', split_axis=0,...  5.66 us
    all_to_all x1, starting transfers between devices, on_device(): lax.all_to_all(mixed.reshape(heads * latents, shards, depth), 'ctx', spli...  4.73 us
    dot_general x4, matrix products, on_device(): jnp.dot(mixed[head * latents:(head + 1) * latents], cross_v[:, cut], pref...  4.18 us
  transfers between devices with their start and end apart: 3, of which 1 were waited for; matrix products, arithmetic and copies ran while one was open for 4% of the time, Pallas kernels for 0%

commit v1 on v0

--- a/solution.py
+++ b/solution.py
@@ -8,6 +8,27 @@
 EPS = 1e-05
 NEG = -1e30
 HEADS_AXES = ("tp", "sub")
+
+
+def ring_gather(x, axis, dim):
+    count, index, span = (lax.axis_size(axis), lax.axis_index(axis), x.shape[dim])
+    right = [(i, (i + 1) % count) for i in range(count)]
+    downward = [(i, (i - 1) % count) for i in range(count)]
+    out = jnp.zeros((*x.shape[:dim], count * span, *x.shape[dim + 1 :]), x.dtype)
+    out = lax.dynamic_update_slice_in_dim(out, x, index * span, axis=dim)
+    from_left = from_right = x
+    half = count // 2
+    for step in range(1, half + 1):
+        from_left = lax.ppermute(from_left, axis, right)
+        out = lax.dynamic_update_slice_in_dim(
+            out, from_left, (index - step) % count * span, axis=dim
+        )
+        if step < count - half:
+            from_right = lax.ppermute(from_right, axis, downward)
+            out = lax.dynamic_update_slice_in_dim(
+                out, from_right, (index + step) % count * span, axis=dim
+            )
+    return out
 
 
 def contract_last(left, right):
@@ -44,7 +65,7 @@
     own = lax.axis_index("ctx")
     mine = lambda array: lax.dynamic_slice_in_dim(array, own * depth, depth, array.ndim - 1)
     whole = lax.all_gather(context, HEADS_AXES, axis=1, tiled=True)
-    all_latents = lax.all_gather(latent_in, "ctx", axis=0, tiled=True).astype(jnp.float32)
+    all_latents = ring_gather(latent_in, "ctx", 0).astype(jnp.float32)
     lat_scale = lax.rsqrt(jnp.mean(all_latents * all_latents, axis=1, keepdims=True) + EPS)
     lat_part = mine(all_latents)
     normed_lat = (lat_part * lat_scale * mine(lat_gain)).astype(jnp.bfloat16)

time: 153 us -> 148 us (0.967)
  blocking collectives: 104 us -> 88.4 us
  waiting for transfers between devices: 6.38 us -> 11.4 us
  starting transfers between devices: 8.01 us -> 11.9 us
    all_gather x1 -> x0, blocking collectives: 15.3 us -> none  [on_device(): lax.all_gather(latent_in, 'ctx', axis=0, tiled=True).astype(jnp.float32)]
    ppermute x0 -> x3, waiting for transfers between devices: none -> 5.68 us  [the longest x2 5.67 us: ring_gather(): from_left = lax.ppermute(from_left, axis, right)]
    ppermute x0 -> x3, starting transfers between devices: none -> 5.11 us  [the longest x2 3.03 us: ring_gather(): from_left = lax.ppermute(from_left, axis, right)]
  transfers between devices with their start and end apart: 3 -> 6, of which waited for: 1 -> 2; matrix products, arithmetic and copies ran while one was open for 4% -> 5% of each run, Pallas kernels for 0% -> 0%
where the time goes in v1:
time: 148 us
  blocking collectives  88.4 us (60%)
  between operations  15 us (10%)
  starting transfers between devices  11.9 us (8%)
  waiting for transfers between devices  11.4 us (8%)
  matrix products  8.52 us (6%)
  local copies, waits for them, and re-layouts  7.2 us (5%)
  other arithmetic  5.33 us (4%)
    all_gather x5, blocking collectives, summed_over(): everything = lax.all_gather(partial.astype(jnp.bfloat16), axis)  53.1 us
    all_gather x1, blocking collectives, on_device(): absorbed = lax.all_gather(absorbed, 'ctx', axis=1, tiled=True)  15.6 us
    all_gather x1, blocking collectives, on_device(): stats = lax.all_gather(jnp.concatenate([top, total], axis=1), 'ctx')  11.3 us
    unnamed x1, blocking collectives  8.34 us
    ppermute x2, waiting for transfers between devices, ring_gather(): from_left = lax.ppermute(from_left, axis, right)  5.67 us
    all_to_all x1, waiting for transfers between devices, on_device(): lax.all_to_all(result.reshape(shards, rows, depth), 'ctx', split_axis=0,...  5.66 us
    dot_general x4, matrix products, on_device(): jnp.dot(mixed[head * latents:(head + 1) * latents], cross_v[:, cut], pref...  4.18 us
    all_to_all x1, starting transfers between devices, on_device(): lax.all_to_all(mixed.reshape(heads * latents, shards, depth), 'ctx', spli...  3.47 us
  transfers between devices with their start and end apart: 6, of which 2 were waited for; matrix products, arithmetic and copies ran while one was open for 5% of the time, Pallas kernels for 0%

profile of v1, /device:TPU:0, one launch (start us, length us, event | category | flops | bytes accessed | tf_op | source)
XLA Modules:
  0.0 147.6 jit_solution(12783981143984140093)
XLA Ops:
  6.5 3.0 %collective-permute-start = (bf16[8,2048]{1,0:T(8,128)(2,1)}, bf16[8,2048]{1,0:T(8,128)(2,1)S(1)}, u32[]{:S(2)}, u32[]{:S(2)}) collective-permute-start(bf16[8,2048]{1,0:T(8,128)(2,1)} %param.15), channel_id=1, source_target_pairs={{0,4},{4,8},{8,12},{12,0},{1,5},{5,9},{9,13},{13,1},{2,6},{6,10},{... | collective-permute-start | bytes 98312 | tf_op jit(solution)/shard_map/ppermute | solution.py:22
  9.6 2.1 %collective-permute-start.1 = (bf16[8,2048]{1,0:T(8,128)(2,1)}, bf16[8,2048]{1,0:T(8,128)(2,1)S(1)}, u32[]{:S(2)}, u32[]{:S(2)}) collective-permute-start(bf16[8,2048]{1,0:T(8,128)(2,1)} %param.15), channel_id=1, source_target_pairs={{0,12},{4,0},{8,4},{12,8},{1,13},{5,1},{9,5},{13,9},{2,14},{6,2},{... | collective-permute-start | bytes 98312 | tf_op jit(solution)/shard_map/ppermute | solution.py:27
  12.4 0.8 constant_dynamic-update-slice_fusion.3
  13.9 0.8 broadcast_multiply_fusion
  15.5 5.7 %collective-permute-done.2 = bf16[8,2048]{1,0:T(8,128)(2,1)S(1)} collective-permute-done((bf16[8,2048]{1,0:T(8,128)(2,1)S(1)}, bf16[8,2048]{1,0:T(8,128)(2,1)S(1)}, u32[]{:S(2)}, u32[]{:S(2)}) %collective-permute-start.2) | collective-permute-done | bytes 32800 | tf_op jit(solution)/shard_map/ppermute | solution.py:22
  21.5 13.4 %all-gather = bf16[128,512]{1,0:T(8,128)(2,1)S(1)} all-gather(bf16[32,512]{1,0:T(8,128)(2,1)S(1)} %convolution_convert_fusion.4), channel_id=2, replica_groups=mesh['grp'=2,'ctx'=4,'tp'=2,'sub'=2] {'ctx'}, dimensions={0}, use_global_device_ids=true | all-gather | bytes 163840 | tf_op jit(solution)/shard_map/all_gather | solution.py:41
  35.6 15.6 %all_gather.48 = bf16[128,2048]{1,0:T(8,128)(2,1)S(1)} all-gather(bf16[128,512]{1,0:T(8,128)(2,1)S(1)} %fusion.14), channel_id=1, replica_groups=mesh['grp'=2,'ctx'=4,'tp'=2,'sub'=2] {'ctx'}, dimensions={1}, use_global_device_ids=true | all-gather | bytes 655360 | tf_op jit(solution)/shard_map/all_gather | solution.py:80
  51.2 1.9 %multiply_reduce_fusion = f32[384]{0:T(512)S(1)} fusion(bf16[384,2048]{1,0:T(8,128)(2,1)} %all-gather.8.cloned.1.call-done), kind=kLoop, calls=%fused_computation | loop fusion | flops 2358912 | bytes 1574400 | tf_op jit(solution)/shard_map/reduce_sum | solution.py:82
  54.9 0.9 copy.17
  55.8 3.5 %all-to-all-start = ((bf16[1,128,4,512]{3,1,0,2:T(8,128)(2,1)}), bf16[1,128,4,512]{3,1,0,2:T(8,128)(2,1)S(1)}, u32[]{:S(2)}, u32[]{:S(2)}) async-start(bf16[1,128,4,512]{3,1,0,2:T(8,128)(2,1)} %copy.17), calls=%async_computation | async-start | bytes 1048576 | tf_op jit(solution)/shard_map/all_to_all | solution.py:95
  59.2 0.8 dynamic_slice.19
  60.0 1.7 %copy.18 = bf16[512,3,512]{0,2,1:T(8,128)(2,1)S(1)} copy(bf16[512,3,512]{2,0,1:T(8,128)(2,1)} %param.24) | data formatting | bytes 3145728 | tf_op args[11]
  63.0 11.3 %all-gather.1 = f32[512,2]{0,1:T(2,128)S(1)} all-gather(f32[128,2]{0,1:T(2,128)S(1)} %pad_maximum_fusion.1), channel_id=3, replica_groups=mesh['grp'=2,'ctx'=4,'tp'=2,'sub'=2] {'ctx'}, dimensions={0}, use_global_device_ids=true | all-gather | bytes 5120 | tf_op jit(solution)/shard_map/all_gather | solution.py:98
  74.7 1.0 fusion.10
  75.8 1.0 fusion.11
  76.8 1.0 fusion.12
  77.9 1.0 fusion.9
  78.9 13.4 %all_gather.52 = bf16[4,32,512]{2,1,0:T(8,128)(2,1)S(1)} all-gather(bf16[1,32,512]{2,1,0:T(8,128)(2,1)S(1)} %pad_maximum_fusion), channel_id=1, replica_groups=mesh['grp'=2,'ctx'=4,'tp'=2,'sub'=2] {'ctx'}, dimensions={0}, use_global_device_ids=true | all-gather | bytes 163840 | tf_op jit(solution)/shard_map/all_gather | solution.py:41
  92.6 5.4 %all-gather.2 = bf16[128,512]{1,0:T(8,128)(2,1)S(1)} all-gather(bf16[32,512]{1,0:T(8,128)(2,1)S(1)} %convolution_convert_fusion.3), channel_id=4, replica_groups=mesh['grp'=2,'ctx'=4,'tp'=2,'sub'=2] {'tp','sub'}, dimensions={0}, use_global_device_ids=true | all-gather | bytes 163840 | tf_op jit(solution)/shard_map/all_gather | solution.py:41
  98.8 15.4 %all-gather.3 = bf16[128,1536]{1,0:T(8,128)(2,1)S(1)} all-gather(bf16[32,1536]{1,0:T(8,128)(2,1)S(1)} %convolution_convert_fusion.1), channel_id=5, replica_groups=mesh['grp'=2,'ctx'=4,'tp'=2,'sub'=2] {'ctx'}, dimensions={0}, use_global_device_ids=true | all-gather | bytes 491520 | tf_op jit(solution)/shard_map/all_gather | solution.py:41
  114.7 8.3 %all-reduce = f32[128]{0:T(128)S(1)} all-reduce(f32[128]{0:T(128)S(1)} %dynamic-update-slice), channel_id=6, replica_groups=mesh['grp'=2,'ctx'=4,'tp'=2,'sub'=2] {'ctx'}, use_global_device_ids=true, to_apply=%add | all-reduce | flops 128 | bytes 1024
  125.1 5.4 %all-gather.5 = bf16[128,512]{1,0:T(8,128)(2,1)S(1)} all-gather(bf16[32,512]{1,0:T(8,128)(2,1)S(1)} %convolution_convert_fusion.2), channel_id=7, replica_groups=mesh['grp'=2,'ctx'=4,'tp'=2,'sub'=2] {'tp','sub'}, dimensions={0}, use_global_device_ids=true | all-gather | bytes 163840 | tf_op jit(solution)/shard_map/all_gather | solution.py:41
  131.2 3.3 %all-to-all-start.1 = ((bf16[4,8,1,512]{3,1,2,0:T(8,128)(2,1)}), bf16[4,8,1,512]{3,1,2,0:T(8,128)(2,1)S(1)}, u32[]{:S(2)}, u32[]{:S(2)}) async-start(bf16[4,8,1,512]{3,1,2,0:T(8,128)(2,1)} %fusion.31), calls=%async_computation.1 | async-start | bytes 65536 | tf_op jit(solution)/shard_map/all_to_all | solution.py:140
  134.5 5.7 %all-to-all-done.1 = bf16[4,8,1,512]{3,1,2,0:T(8,128)(2,1)S(1)} async-done(((bf16[4,8,1,512]{3,1,2,0:T(8,128)(2,1)}), bf16[4,8,1,512]{3,1,2,0:T(8,128)(2,1)S(1)}, u32[]{:S(2)}, u32[]{:S(2)}) %all-to-all-start.1) | async-done | bytes 32800 | tf_op jit(solution)/shard_map/all_to_all | solution.py:140
  (80 shorter events, 10.1 us)
Async XLA Ops:
  6.5 14.8 %copy-start = (bf16[512,512]{1,0:T(8,128)(2,1)S(1)}, bf16[512,512]{1,0:T(8,128)(2,1)}, u32[]{:S(2)}) copy-start(bf16[512,512]{1,0:T(8,128)(2,1)} %param.20) | copy-start | bytes 1572868
  6.5 28.4 %copy-start.4 = (bf16[512,512]{1,0:T(8,128)(2,1)S(1)}, bf16[512,512]{1,0:T(8,128)(2,1)}, u32[]{:S(2)}) copy-start(bf16[512,512]{1,0:T(8,128)(2,1)} %param.21) | copy-start | bytes 1572868
  6.5 44.7 %all-gather.8.cloned.1.call-start = ((), (), s32[]{:S(2)}) async-start(), calls=%async_computation.2 | async-start | bytes 1966080 | tf_op jit(solution)/shard_map/all_gather | solution.py:67
  6.5 8.9 %collective-permute-start = (bf16[8,2048]{1,0:T(8,128)(2,1)}, bf16[8,2048]{1,0:T(8,128)(2,1)S(1)}, u32[]{:S(2)}, u32[]{:S(2)}) collective-permute-start(bf16[8,2048]{1,0:T(8,128)(2,1)} %param.15), channel_id=1, source_target_pairs={{0,4},{4,8},{8,12},{12,0},{1,5},{5,9},{9,13},{13,1},{2,6},{6,10},{... | collective-permute-start | bytes 98312 | tf_op jit(solution)/shard_map/ppermute | solution.py:22
  9.6 5.9 %collective-permute-start.1 = (bf16[8,2048]{1,0:T(8,128)(2,1)}, bf16[8,2048]{1,0:T(8,128)(2,1)S(1)}, u32[]{:S(2)}, u32[]{:S(2)}) collective-permute-start(bf16[8,2048]{1,0:T(8,128)(2,1)} %param.15), channel_id=1, source_target_pairs={{0,12},{4,0},{8,4},{12,8},{1,13},{5,1},{9,5},{13,9},{2,14},{6,2},{... | collective-permute-start | bytes 98312 | tf_op jit(solution)/shard_map/ppermute | solution.py:27
  15.4 5.7 %collective-permute-start.2 = (bf16[8,2048]{1,0:T(8,128)(2,1)S(1)}, bf16[8,2048]{1,0:T(8,128)(2,1)S(1)}, u32[]{:S(2)}, u32[]{:S(2)}) collective-permute-start(bf16[8,2048]{1,0:T(8,128)(2,1)S(1)} %collective-permute-done), channel_id=1, source_target_pairs={{0,4},{4,8},{8,12},{12,0},{1,5},{5,9},{9,13},{13,1},{2,6},{6,10},{... | collective-permute-start | bytes 98312 | tf_op jit(solution)/shard_map/ppermute | solution.py:22
  51.2 1.9 %copy-start.1 = (bf16[384,2048]{1,0:T(8,128)(2,1)S(1)}, bf16[384,2048]{1,0:T(8,128)(2,1)}, u32[]{:S(2)}) copy-start(bf16[384,2048]{1,0:T(8,128)(2,1)} %all-gather.8.cloned.1.call-done) | copy-start | bytes 4718596
  55.8 18.7 %all-to-all-start = ((bf16[1,128,4,512]{3,1,0,2:T(8,128)(2,1)}), bf16[1,128,4,512]{3,1,0,2:T(8,128)(2,1)S(1)}, u32[]{:S(2)}, u32[]{:S(2)}) async-start(bf16[1,128,4,512]{3,1,0,2:T(8,128)(2,1)} %copy.17), calls=%async_computation | async-start | bytes 1048576 | tf_op jit(solution)/shard_map/all_to_all | solution.py:95
  60.0 1.8 %copy-start.5 = (u32[32]{0:T(128)S(1)}, u32[32]{0:T(128)}, u32[]{:S(2)}) copy-start(u32[32]{0:T(128)} %constant.76) | copy-start | bytes 388
  61.8 30.6 %copy-start.2 = (bf16[512,512]{1,0:T(8,128)(2,1)S(1)}, bf16[512,512]{1,0:T(8,128)(2,1)}, u32[]{:S(2)}) copy-start(bf16[512,512]{1,0:T(8,128)(2,1)} %param.23) | copy-start | bytes 1572868
  98.7 26.1 %copy-start.3 = (bf16[512,512]{1,0:T(8,128)(2,1)S(1)}, bf16[512,512]{1,0:T(8,128)(2,1)}, u32[]{:S(2)}) copy-start(bf16[512,512]{1,0:T(8,128)(2,1)} %param.25) | copy-start | bytes 1572868
  131.2 8.9 %all-to-all-start.1 = ((bf16[4,8,1,512]{3,1,2,0:T(8,128)(2,1)}), bf16[4,8,1,512]{3,1,2,0:T(8,128)(2,1)S(1)}, u32[]{:S(2)}, u32[]{:S(2)}) async-start(bf16[4,8,1,512]{3,1,2,0:T(8,128)(2,1)} %fusion.31), calls=%async_computation.1 | async-start | bytes 65536 | tf_op jit(solution)/shard_map/all_to_all | solution.py:140
Sparse Core Ops, SparseCore 0:
  11.8 19.4 all-gather.7
